TPU v7x, 32 devices: a whole 2x2x4 slice. The times are simulated.
32 devices in a mesh: row: 8 (over y, x, core), col: 4 (over z).
Axes of the slice: x: 2, y: 2, z: 4, core: 2. Of those that a mesh axis runs over, the one named last changes fastest.
Arguments:
- panel: int32 [32], replicated, may hold values from 0 to 31, each once
- trailing: float32 [8192, 8192], P('row', 'col'), as said below
Outputs:
- factor_panels: float32 [8192, 768], P('row')
- schur: float32 [8192, 8192], P('row', 'col')
Inputs may be any that keep to these rules, and one draw needn't show every extreme that they name: panel names every block index once. In matrix order trailing is symmetric, and each diagonal block of 256 x 256 is strictly diagonally dominant with a positive diagonal.
All inputs are finite; a program needn't handle non-finite values.
Results may differ from a plain program's by a relative error of at most 0.0001.
Values sent between devices are 32-bit elements; how exact they have to be, the bound alone decides.
No kernel may reach another device: no remote copies, remote signals or barrier semaphores. Data moves between devices by JAX's collectives and lax.ppermute only.
A program may use at most 128 MiB of HBM per device.

v0:
```python
import jax
import jax.numpy as jnp
from jax import lax
from jax.sharding import PartitionSpec as P

NB = 256
PANELS = 3


def spread(value, axis, source):
    kept = jnp.where(lax.axis_index(axis) == source, value, 0).astype(value.dtype)
    return lax.psum(kept, axis)


def solve_panel(columns, corner):
    lower = jnp.linalg.cholesky(corner)
    identity = jnp.eye(corner.shape[0], dtype=jnp.float32)
    inverse = lax.linalg.triangular_solve(lower, identity, left_side=True, lower=True)
    return jnp.dot(
        columns, inverse.T, precision=lax.Precision.HIGHEST, preferred_element_type=jnp.float32
    )


def on_device(panel, trailing):
    rows_all = lax.axis_size("row")
    cols_all = lax.axis_size("col")
    my_row = lax.axis_index("row")
    my_col = lax.axis_index("col")
    loc_rows, loc_cols = trailing.shape
    blk_rows = loc_rows // NB
    blk_cols = loc_cols // NB
    ratio = rows_all // cols_all
    row_ids = jnp.arange(loc_rows, dtype=jnp.int32) // NB
    col_ids = jnp.arange(loc_cols, dtype=jnp.int32) // NB
    current = trailing
    factors = []
    for step in range(PANELS):
        pivot = panel[step]
        owner_row = pivot % rows_all
        local_row = pivot // rows_all
        owner_col = pivot % cols_all
        local_col = pivot // cols_all
        columns = lax.dynamic_slice_in_dim(current, local_col * NB, NB, 1)
        corner = lax.dynamic_slice_in_dim(columns, local_row * NB, NB, 0)
        pivot_tile = spread(corner, "row", owner_row)
        row_factor = spread(solve_panel(columns, pivot_tile), "col", owner_col)
        pieces = []
        for offset in range(ratio):
            fetched = spread(row_factor, "row", my_col + offset * cols_all)
            pieces.append(fetched.reshape(blk_rows, NB, NB))
        col_factor = jnp.stack(pieces, axis=1).reshape(blk_cols * NB, NB)
        update = lax.dot_general(
            row_factor,
            col_factor,
            (((1,), (1,)), ((), ())),
            precision=lax.Precision.HIGHEST,
            preferred_element_type=jnp.float32,
        )
        current = current - update
        keep_rows = (row_ids != local_row) | (my_row != owner_row)
        keep_cols = (col_ids != local_col) | (my_col != owner_col)
        current = jnp.where(keep_rows[:, None] & keep_cols[None, :], current, jnp.float32(0.0))
        factors.append(row_factor)
    return (jnp.concatenate(factors, axis=1), current)


def solution(mesh):
    in_specs = (P(), P("row", "col"))
    out_specs = (P("row", None), P("row", "col"))
    return jax.shard_map(
        on_device, mesh=mesh, in_specs=in_specs, out_specs=out_specs, check_vma=False
    )
```

profile of v0, /device:TPU:3, one launch (start us, length us, event | category | flops | bytes accessed | tf_op | source)
XLA Modules:
  0.0 794.5 jit_solution(4477696324197038148)
XLA Ops:
  7.2 1.4 fusion.64
  11.3 9.3 %copy.13 = f32[1024,2048]{0,1:T(8,128)} copy(f32[1024,2048]{1,0:T(8,128)} %param.6) | data formatting | bytes 16777216 | tf_op args[1]
  20.5 1.8 dynamic-slice_select_fusion.2
  22.5 53.5 %all-reduce.14.cloned.1.call-done = f32[256,256]{0,1:T(8,128)} async-done(((f32[256,256]{0,1:T(8,128)}), f32[256,256]{0,1:T(8,128)}) %all-reduce.14.cloned.1.call-update) | async-done | bytes 262160 | tf_op jit(solution)/shard_map/psum | solution.py:12
  76.0 1.1 copy.14
  77.1 1.0 fusion.14
  78.1 11.7 %cholesky.172 = f32[128,128]{1,0:T(8,128)S(1)} custom-call(f32[128,128]{1,0:T(8,128)S(1)} %cholesky.270), custom_call_target="Cholesky" | custom-call | tf_op jit(solution)/shard_map/jit(cholesky)/cholesky | solution.py:16
  89.9 9.8 %custom-call.15 = f32[1,128,128]{1,2,0:T(8,128)S(1)} custom-call(f32[1,128,128]{2,1,0:T(8,128)S(1)} %get-tuple-element.84), custom_call_target="InvertDiagBlocksLowerTriangular" | custom-call | tf_op jit(solution)/shard_map/jit(cholesky)/cholesky | solution.py:16
  100.2 11.7 %cholesky.189 = f32[128,128]{1,0:T(8,128)S(1)} custom-call(f32[128,128]{1,0:T(8,128)S(1)} %convolution_subtract_fusion.5), custom_call_target="Cholesky" | custom-call | tf_op jit(solution)/shard_map/jit(cholesky)/cholesky | solution.py:16
  111.9 0.7 compare_reduce_fusion.4
  114.1 4.3 while.6
  114.4 0.6 fusion.86
  115.0 1.4 bitcast_dynamic-update-slice_fusion.6
  116.4 0.6 fusion.86
  117.0 1.4 bitcast_dynamic-update-slice_fusion.6
  118.4 19.7 %custom-call.16 = f32[2,128,128]{1,2,0:T(8,128)S(1)} custom-call(f32[2,128,128]{2,1,0:T(8,128)S(1)} %get-tuple-element.24), custom_call_target="InvertDiagBlocksLowerTriangular" | custom-call | tf_op jit(solution)/shard_map/triangular_solve/custom-call.0 | solution.py:18
  139.0 3.2 convolution_select_fusion.2
  142.3 53.1 %all-reduce.16.cloned.1.call-done = f32[1024,256]{1,0:T(8,128)} async-done(((f32[1024,256]{1,0:T(8,128)}), f32[1024,256]{1,0:T(8,128)}) %all-reduce.16.cloned.1.call-update) | async-done | bytes 1048592 | tf_op jit(solution)/shard_map/psum | solution.py:12
  195.5 2.7 broadcast_select_fusion.5
  201.2 57.4 %all-reduce.30.cloned.1.call-done = (f32[4,1,256,256]{3,2,1,0:T(8,128)}, f32[4,1,256,256]{3,2,1,0:T(8,128)}) async-done(((f32[4,1,256,256]{3,2,1,0:T(8,128)}, f32[4,1,256,256]{3,2,1,0:T(8,128)}), (f32[4,1,256,256]{3,2,1,0:T(8,128)}, f32[4,1,256,256]{3,2,1,0:T(8,128)})) %all-reduce.30.cloned.1.call-update) | async-done | bytes 2097168 | tf_op jit(solution)/shard_map/psum | solution.py:12
  258.5 1.8 pad_maximum_fusion.1
  260.3 10.4 %subtract_select_fusion.2 = f32[1024,2048]{0,1:T(8,128)S(1)} fusion(f32[1024,2048]{0,1:T(8,128)} %copy.13, f32[1024,256]{1,0:T(8,128)S(1)} %copy-done.2, f32[2048,256]{1,0:T(8,128)S(1)} %bitcast.124, pred[1024]{0:T(1024)(128)(4,1)S(1)} %fusion.51, pred[2048]{0:T(1024)(128)(4,1)S(1)} %fusion.42), kind=kOutput, calls=%fused_computation.8 | convolution fusion | flops 6448742400 | bytes 19926016 | tf_op jit(solution)/shard_map/dot_general | solution.py:52
  270.7 3.4 copy-done
  274.1 0.8 dynamic-slice_select_fusion.1
  275.4 52.8 %all-reduce.18.cloned.1.call-done = f32[256,256]{0,1:T(8,128)} async-done(((f32[256,256]{0,1:T(8,128)}), f32[256,256]{0,1:T(8,128)}) %all-reduce.18.cloned.1.call-update) | async-done | bytes 262160 | tf_op jit(solution)/shard_map/psum | solution.py:12
  328.2 1.1 copy.19
  329.3 1.0 fusion.13
  330.3 11.7 %cholesky.206 = f32[128,128]{1,0:T(8,128)S(1)} custom-call(f32[128,128]{1,0:T(8,128)S(1)} %cholesky.273), custom_call_target="Cholesky" | custom-call | tf_op jit(solution)/shard_map/jit(cholesky)/cholesky | solution.py:16
  342.0 0.6 compare_reduce_fusion.3
  342.7 9.8 %custom-call.17 = f32[1,128,128]{1,2,0:T(8,128)S(1)} custom-call(f32[1,128,128]{2,1,0:T(8,128)S(1)} %get-tuple-element.80), custom_call_target="InvertDiagBlocksLowerTriangular" | custom-call | tf_op jit(solution)/shard_map/jit(cholesky)/cholesky | solution.py:16
  353.0 11.7 %cholesky.223 = f32[128,128]{1,0:T(8,128)S(1)} custom-call(f32[128,128]{1,0:T(8,128)S(1)} %convolution_subtract_fusion.4), custom_call_target="Cholesky" | custom-call | tf_op jit(solution)/shard_map/jit(cholesky)/cholesky | solution.py:16
  364.8 0.7 compare_reduce_fusion.2
  366.9 4.3 while.7
  367.7 1.4 bitcast_dynamic-update-slice_fusion.7
  369.7 1.4 bitcast_dynamic-update-slice_fusion.7
  371.2 19.7 %custom-call.18 = f32[2,128,128]{1,2,0:T(8,128)S(1)} custom-call(f32[2,128,128]{2,1,0:T(8,128)S(1)} %get-tuple-element.25), custom_call_target="InvertDiagBlocksLowerTriangular" | custom-call | tf_op jit(solution)/shard_map/triangular_solve/custom-call.0 | solution.py:18
  391.7 4.0 convolution_select_fusion.1
  395.8 53.1 %all-reduce.20.cloned.1.call-done = f32[1024,256]{1,0:T(8,128)} async-done(((f32[1024,256]{1,0:T(8,128)}), f32[1024,256]{1,0:T(8,128)}) %all-reduce.20.cloned.1.call-update) | async-done | bytes 1048592 | tf_op jit(solution)/shard_map/psum | solution.py:12
  449.0 2.7 broadcast_select_fusion.3
  454.3 57.6 %all-reduce.28.cloned.1.call-done = (f32[4,1,256,256]{3,2,1,0:T(8,128)}, f32[4,1,256,256]{3,2,1,0:T(8,128)}) async-done(((f32[4,1,256,256]{3,2,1,0:T(8,128)}, f32[4,1,256,256]{3,2,1,0:T(8,128)}), (f32[4,1,256,256]{3,2,1,0:T(8,128)}, f32[4,1,256,256]{3,2,1,0:T(8,128)})) %all-reduce.28.cloned.1.call-update) | async-done | bytes 2097168 | tf_op jit(solution)/shard_map/psum | solution.py:12
  511.9 1.8 pad_maximum_fusion.2
  513.7 10.4 %subtract_select_fusion.1 = f32[1024,2048]{0,1:T(8,128)S(1)} fusion(f32[1024,2048]{0,1:T(8,128)} %copy-done, f32[1024,256]{1,0:T(8,128)S(1)} %copy-done.3, f32[2048,256]{1,0:T(8,128)S(1)} %bitcast.125, pred[1024]{0:T(1024)(128)(4,1)S(1)} %fusion.52, pred[2048]{0:T(1024)(128)(4,1)S(1)} %fusion.43), kind=kOutput, calls=%fused_computation.7 | convolution fusion | flops 6448742400 | bytes 19926016 | tf_op jit(solution)/shard_map/dot_general | solution.py:52
  524.1 3.4 copy-done.1
  527.5 0.8 dynamic-slice_select_fusion
  528.6 53.0 %all-reduce.22.cloned.1.call-done = f32[256,256]{0,1:T(8,128)} async-done(((f32[256,256]{0,1:T(8,128)}), f32[256,256]{0,1:T(8,128)}) %all-reduce.22.cloned.1.call-update) | async-done | bytes 262160 | tf_op jit(solution)/shard_map/psum | solution.py:12
  581.6 1.1 copy.23
  582.7 1.0 fusion.12
  583.7 11.7 %cholesky.240 = f32[128,128]{1,0:T(8,128)S(1)} custom-call(f32[128,128]{1,0:T(8,128)S(1)} %cholesky.276), custom_call_target="Cholesky" | custom-call | tf_op jit(solution)/shard_map/jit(cholesky)/cholesky | solution.py:16
  595.4 0.6 compare_reduce_fusion.1
  596.1 9.8 %custom-call.19 = f32[1,128,128]{1,2,0:T(8,128)S(1)} custom-call(f32[1,128,128]{2,1,0:T(8,128)S(1)} %get-tuple-element.76), custom_call_target="InvertDiagBlocksLowerTriangular" | custom-call | tf_op jit(solution)/shard_map/jit(cholesky)/cholesky | solution.py:16
  606.4 11.7 %cholesky.257 = f32[128,128]{1,0:T(8,128)S(1)} custom-call(f32[128,128]{1,0:T(8,128)S(1)} %convolution_subtract_fusion.3), custom_call_target="Cholesky" | custom-call | tf_op jit(solution)/shard_map/jit(cholesky)/cholesky | solution.py:16
  618.1 0.7 compare_reduce_fusion
  620.2 4.4 while.8
  621.1 1.4 bitcast_dynamic-update-slice_fusion.8
  623.2 1.4 bitcast_dynamic-update-slice_fusion.8
  624.6 19.7 %custom-call.20 = f32[2,128,128]{1,2,0:T(8,128)S(1)} custom-call(f32[2,128,128]{2,1,0:T(8,128)S(1)} %get-tuple-element.26), custom_call_target="InvertDiagBlocksLowerTriangular" | custom-call | tf_op jit(solution)/shard_map/triangular_solve/custom-call.0 | solution.py:18
  645.2 4.0 convolution_select_fusion
  649.3 53.1 %all-reduce.24.cloned.1.call-done = f32[1024,256]{1,0:T(8,128)} async-done(((f32[1024,256]{1,0:T(8,128)}), f32[1024,256]{1,0:T(8,128)}) %all-reduce.24.cloned.1.call-update) | async-done | bytes 1048592 | tf_op jit(solution)/shard_map/psum | solution.py:12
  702.4 2.8 broadcast_select_fusion.1
  705.3 1.9 pad_maximum_fusion
  707.2 57.7 %all-reduce.26.cloned.1.call-done = (f32[4,1,256,256]{3,2,1,0:T(8,128)}, f32[4,1,256,256]{3,2,1,0:T(8,128)}) async-done(((f32[4,1,256,256]{3,2,1,0:T(8,128)}, f32[4,1,256,256]{3,2,1,0:T(8,128)}), (f32[4,1,256,256]{3,2,1,0:T(8,128)}, f32[4,1,256,256]{3,2,1,0:T(8,128)})) %all-reduce.26.cloned.1.call-update) | async-done | bytes 2097168 | tf_op jit(solution)/shard_map/psum | solution.py:12
  764.9 1.8 pad_maximum_fusion.3
  766.7 11.7 %subtract_select_fusion = f32[1024,2048]{0,1:T(8,128)} fusion(f32[1024,2048]{0,1:T(8,128)} %copy-done.1, f32[1024,256]{1,0:T(8,128)S(1)} %copy-done.4, f32[2048,256]{1,0:T(8,128)S(1)} %bitcast.123, pred[1024]{0:T(1024)(128)(4,1)S(1)} %fusion.53, pred[2048]{0:T(1024)(128)(4,1)S(1)} %fusion.44), kind=kOutput, calls=%fused_computation.6 | convolution fusion | flops 6448742400 | bytes 19926016 | tf_op jit(solution)/shard_map/dot_general | solution.py:52
  778.4 9.1 %copy.27 = f32[1024,2048]{1,0:T(8,128)} copy(f32[1024,2048]{0,1:T(8,128)} %subtract_select_fusion) | data formatting | bytes 16777216
  (78 shorter events, 8.2 us)
Async XLA Ops:
  7.2 68.9 %all-reduce.14.cloned.1.call-start = ((), (), s32[]{:S(2)}) async-start(), calls=%async_computation | async-start | bytes 524288 | tf_op jit(solution)/shard_map/psum | solution.py:12
  22.4 173.1 %all-reduce.16.cloned.1.call-start = ((), (), s32[]{:S(2)}) async-start(), calls=%async_computation.1 | async-start | bytes 2097152 | tf_op jit(solution)/shard_map/psum | solution.py:12
  142.3 116.2 %all-reduce.30.cloned.1.call-start = ((), (), s32[]{:S(2)}) async-start(), calls=%async_computation.8 | async-start | bytes 4194304 | tf_op jit(solution)/shard_map/psum | solution.py:12
  198.2 62.1 %copy-start.2 = (f32[1024,256]{1,0:T(8,128)S(1)}, f32[1024,256]{1,0:T(8,128)}, u32[]{:S(2)}) copy-start(f32[1024,256]{1,0:T(8,128)} %all-reduce.16.cloned.1.call-done) | copy-start | bytes 3145732
  198.2 130.0 %all-reduce.18.cloned.1.call-start = ((), (), s32[]{:S(2)}) async-start(), calls=%async_computation.2 | async-start | bytes 524288 | tf_op jit(solution)/shard_map/psum | solution.py:12
  270.7 3.4 copy-start
  274.9 174.0 %all-reduce.20.cloned.1.call-start = ((), (), s32[]{:S(2)}) async-start(), calls=%async_computation.3 | async-start | bytes 2097152 | tf_op jit(solution)/shard_map/psum | solution.py:12
  395.8 116.1 %all-reduce.28.cloned.1.call-start = ((), (), s32[]{:S(2)}) async-start(), calls=%async_computation.7 | async-start | bytes 4194304 | tf_op jit(solution)/shard_map/psum | solution.py:12
  451.7 62.0 %copy-start.3 = (f32[1024,256]{1,0:T(8,128)S(1)}, f32[1024,256]{1,0:T(8,128)}, u32[]{:S(2)}) copy-start(f32[1024,256]{1,0:T(8,128)} %all-reduce.20.cloned.1.call-done) | copy-start | bytes 3145732
  451.7 129.9 %all-reduce.22.cloned.1.call-start = ((), (), s32[]{:S(2)}) async-start(), calls=%async_computation.4 | async-start | bytes 524288 | tf_op jit(solution)/shard_map/psum | solution.py:12
  524.1 3.4 copy-start.1
  528.3 174.1 %all-reduce.24.cloned.1.call-start = ((), (), s32[]{:S(2)}) async-start(), calls=%async_computation.5 | async-start | bytes 2097152 | tf_op jit(solution)/shard_map/psum | solution.py:12
  649.2 115.7 %all-reduce.26.cloned.1.call-start = ((), (), s32[]{:S(2)}) async-start(), calls=%async_computation.6 | async-start | bytes 4194304 | tf_op jit(solution)/shard_map/psum | solution.py:12
  702.4 2.9 copy-start.4
Sparse Core Ops, SparseCore 0:
  22.5 53.4 all-reduce.13
  142.4 53.0 all-reduce.15
  199.3 59.1 all-reduce.29
  275.1 53.0 all-reduce.17
  395.9 53.0 all-reduce.19
  452.7 59.1 all-reduce.27
  528.4 53.0 all-reduce.21
  649.4 53.0 all-reduce.23
  705.7 59.1 all-reduce.25
where the time goes:
time: 807 us; the launch traced here: 795 us
  waiting for transfers between devices  491 us (61%)
  other arithmetic  184 us (23%)
  matrix products  47.7 us (6%)
  local copies, waits for them, and re-layouts  42.2 us (5%)
  between operations  26.9 us (3%)
    psum x9, waiting for transfers between devices, spread(): return lax.psum(kept, axis)  491 us
    another operation x20, other arithmetic, solve_panel(): lower = jnp.linalg.cholesky(corner)  103 us
    another operation x7, other arithmetic, solve_panel(): lax.linalg.triangular_solve(lower, identity, left_side=True, lower=True)  59.1 us
    dot_general x3, matrix products, on_device(): lax.dot_general(row_factor, col_factor, (((1,), (1,)), ((), ())), precisi...  32.4 us
    unnamed x12, local copies, waits for them, and re-layouts  25.2 us
  transfers between devices with their start and end apart: 9, of which 9 were waited for; matrix products, arithmetic and copies ran while one was open for 0% of the time, Pallas kernels for 0%

commit v1 on v0

v1 whole, which is shorter than its diff:
```python
import jax
import jax.numpy as jnp
from jax import lax
from jax.sharding import PartitionSpec as P

NB = 256
PANELS = 3
AXES = ("row", "col")
HIGHEST = lax.Precision.HIGHEST


def mm(a, b, dims=((1,), (0,)), precision=HIGHEST):
    return lax.dot_general(
        a, b, (dims, ((), ())), precision=precision, preferred_element_type=jnp.float32
    )


class Net:
    def __init__(self, rows, cols):
        self.rows, self.cols = rows, cols
        self.row_bits = [1 << i for i in range(1, rows.bit_length() - 1)]
        self.col_bits = [1 << i for i in range(cols.bit_length() - 1)]

    def send(self, value, target):
        pairs = []
        for r in range(self.rows):
            for c in range(self.cols):
                to = target(r, c)
                if to is not None:
                    pairs.append((r * self.cols + c, to[0] * self.cols + to[1]))
        return lax.ppermute(value, AXES, pairs)

    def core(self, value):
        return self.send(value, lambda r, c: (r ^ 1, c))

    def row_step(self, value, step):
        bits = self.row_bits
        count = len(bits)
        return self.send(
            value, lambda r, c: (r ^ bits[(step + (r & 1)) % count], c)
        )

    def col_step(self, value, bit):
        return self.send(value, lambda r, c: (r, c ^ bit))

    def row_halves(self, value, mine):
        keep = lax.dynamic_index_in_dim(value, mine, 0, keepdims=False)
        give = lax.dynamic_index_in_dim(value, 1 - mine, 0, keepdims=False)
        half = keep + self.core(give)
        for step in range(len(self.row_bits)):
            half = half + self.row_step(half, step)
        return half

    def join(self, half, mine):
        other = self.core(half)
        first = jnp.where(mine == 0, half, other)
        second = jnp.where(mine == 0, other, half)
        return jnp.stack([first, second])


def spread_rows(net, source, is_source):
    if (net.rows, net.cols) != (8, 4):
        value = jnp.where(is_source, source, 0.0)
        for bit in net.col_bits:
            value = value + net.col_step(value, bit)
        return value

    def hop(first, second):
        def target(r, c):
            up = (r // 2) % 2 == 0
            line = c if up else 3 - c
            near = (r % 2 == 0) == up
            to = (first if near else second).get(line)
            if to is None:
                return None
            return (r, to if up else 3 - to)

        return target

    got1 = net.send(source, hop({0: 1}, {1: 2}))
    got2 = net.send(got1, hop({1: 2}, {2: 3}))
    got3 = net.send(jnp.where(is_source, source, got2), hop({2: 3}, {1: 0}))
    return jnp.where(is_source, source, got1 + got2 + got3)


def invert(corner):
    lower = jnp.linalg.cholesky(corner)
    identity = jnp.eye(corner.shape[0], dtype=jnp.float32)
    return lax.linalg.triangular_solve(lower, identity, left_side=True, lower=True)


def on_device(panel, trailing):
    rows = lax.axis_size("row")
    cols = lax.axis_size("col")
    my_row = lax.axis_index("row")
    my_col = lax.axis_index("col")
    net = Net(rows, cols)
    mine = my_row % 2
    loc_rows, loc_cols = trailing.shape
    blk_rows = loc_rows // NB
    blk_cols = loc_cols // NB
    ratio = rows // cols

    strips = []
    for s in range(PANELS):
        pivot = panel[s]
        strip = lax.dynamic_slice_in_dim(trailing, (pivot // rows) * NB, NB, 0)
        strips.append(jnp.where(my_row == pivot % rows, strip, 0.0))

    blocks = []
    names = []
    for a in range(PANELS):
        for b in range(a + 1):
            piece = lax.dynamic_slice_in_dim(strips[a], (panel[b] // cols) * NB, NB, 1)
            blocks.append(jnp.where(my_col == panel[b] % cols, piece, 0.0))
            names.append((a, b))
    packed = jnp.stack(blocks).reshape(2, len(blocks) // 2, NB, NB)
    half = net.row_halves(packed, mine)
    for bit in net.col_bits:
        half = half + net.col_step(half, bit)
    packed = net.join(half, mine).reshape(len(blocks), NB, NB)
    corner = {name: packed[i] for i, name in enumerate(names)}

    is_source = my_col == my_row % cols
    col_raw, row_raw = [], []
    for s in range(PANELS):
        strip = strips[s].reshape(2, NB // 2, loc_cols)
        full = net.join(net.row_halves(strip, mine), mine).reshape(NB, loc_cols)
        col_raw.append(full)
        own = full.reshape(NB, blk_rows, ratio, NB)
        own = lax.dynamic_index_in_dim(own, my_row // cols, 2, keepdims=False)
        row_raw.append(spread_rows(net, own.reshape(NB, loc_rows), is_source))

    inverse, low = [], {}
    for s in range(PANELS):
        diag = corner[(s, s)]
        for k in range(s):
            diag = diag - mm(low[(s, k)], low[(s, k)], ((1,), (1,)))
        inverse.append(invert(diag))
        for a in range(s + 1, PANELS):
            left = corner[(a, s)]
            for k in range(s):
                left = left - mm(low[(a, k)], low[(s, k)], ((1,), (1,)))
            low[(a, s)] = mm(left, inverse[s], ((1,), (1,)))

    row_ids = jnp.arange(loc_rows, dtype=jnp.int32) // NB * rows + my_row
    col_ids = jnp.arange(loc_cols, dtype=jnp.int32) // NB * cols + my_col

    def factors(raw, ids):
        out = []
        alive = jnp.ones(ids.shape, jnp.bool_)
        for s in range(PANELS):
            left = raw[s]
            for k in range(s):
                left = left - mm(low[(s, k)], out[k])
            out.append(jnp.where(alive[None, :], mm(inverse[s], left), 0.0))
            alive = alive & (ids != panel[s])
        return out, alive

    row_factor, row_alive = factors(row_raw, row_ids)
    col_factor, col_alive = factors(col_raw, col_ids)
    row_all = jnp.concatenate(row_factor, axis=0).T
    col_all = jnp.concatenate(col_factor, axis=0)
    current = trailing - mm(row_all, col_all)
    current = jnp.where(row_alive[:, None] & col_alive[None, :], current, 0.0)
    return (row_all, current)


def solution(mesh):
    in_specs = (P(), P("row", "col"))
    out_specs = (P("row", None), P("row", "col"))
    return jax.shard_map(
        on_device, mesh=mesh, in_specs=in_specs, out_specs=out_specs, check_vma=False
    )
```

time: 807 us -> 513 us (0.64)
  waiting for transfers between devices: 491 us -> 130 us
  starting transfers between devices: 0.99 us -> 31.3 us
  other arithmetic: 184 us -> 204 us
  local copies, waits for them, and re-layouts: 42.2 us -> 60.5 us
  matrix products: 47.7 us -> 64.5 us
  between operations: 26.9 us -> 13.6 us
    psum x9 -> x0, waiting for transfers between devices: 491 us -> none  [spread(): return lax.psum(kept, axis)]
    ppermute x0 -> x27, waiting for transfers between devices: none -> 130 us  [send(): return lax.ppermute(value, AXES, pairs)]
    ppermute x0 -> x27, starting transfers between devices: none -> 31.3 us  [send(): return lax.ppermute(value, AXES, pairs)]
    dynamic_slice x0 -> x5, local copies, waits for them, and re-layouts: none -> 19.5 us  [the longest x2 13.6 us: on_device(): own = lax.dynamic_index_in_dim(own, my_row // cols, 2, keepdims=False)]
    dot_general x6 -> x20, matrix products: 43.7 us -> 60.5 us  [mm(): lax.dot_general(a, b, (dims, ((), ())), precision=precision, preferred_el...]
    unnamed x12 -> x68, local copies, waits for them, and re-layouts: 25.2 us -> 10.9 us
    add x0 -> x14, other arithmetic: none -> 13.6 us  [the longest x4 5.82 us: row_halves(): half = keep + self.core(give)]
    another operation x28 -> x31, local copies, waits for them, and re-layouts: 12.4 us -> 23.6 us  [the longest x22 15.2 us: invert(): lax.linalg.triangular_solve(lower, identity, left_side=True, lower=True)]
  transfers between devices with their start and end apart: 9 -> 27, of which waited for: 9 -> 9; matrix products, arithmetic and copies ran while one was open for 0% -> 55% of each run, Pallas kernels for 0% -> 0%
where the time goes in v1:
time: 513 us; the launch traced here: 504 us
  other arithmetic  204 us (40%)
  waiting for transfers between devices  130 us (25%)
  matrix products  64.5 us (13%)
  local copies, waits for them, and re-layouts  60.5 us (12%)
  starting transfers between devices  31.3 us (6%)
  between operations  13.6 us (3%)
    ppermute x27, waiting for transfers between devices, send(): return lax.ppermute(value, AXES, pairs)  130 us
    another operation x20, other arithmetic, invert(): lower = jnp.linalg.cholesky(corner)  104 us
    another operation x7, other arithmetic, invert(): lax.linalg.triangular_solve(lower, identity, left_side=True, lower=True)  61 us
    dot_general x20, matrix products, mm(): lax.dot_general(a, b, (dims, ((), ())), precision=precision, preferred_el...  60.5 us
    ppermute x27, starting transfers between devices, send(): return lax.ppermute(value, AXES, pairs)  31.3 us
    another operation x22, local copies, waits for them, and re-layouts, invert(): lax.linalg.triangular_solve(lower, identity, left_side=True, lower=True)  15.2 us
    dynamic_slice x2, local copies, waits for them, and re-layouts, on_device(): own = lax.dynamic_index_in_dim(own, my_row // cols, 2, keepdims=False)  13.6 us
    unnamed x68, local copies, waits for them, and re-layouts  10.9 us
  transfers between devices with their start and end apart: 27, of which 9 were waited for; matrix products, arithmetic and copies ran while one was open for 55% of the time, Pallas kernels for 0%

profile of v1, /device:TPU:3, one launch (start us, length us, event | category | flops | bytes accessed | tf_op | source)
XLA Modules:
  0.0 504.1 jit_solution(4019278257854557801)
XLA Ops:
  0.6 1.4 fusion.87
  9.8 3.5 dynamic-slice_select_fusion
  16.0 1.7 bitcast_dynamic-update-slice_fusion.6
  19.9 2.4 constant_dynamic-slice_fusion.4
  22.3 2.3 copy.5
  25.3 2.4 dynamic-slice_bitcast_fusion.2
  31.6 1.6 bitcast_add_fusion.3
  36.3 1.5 bitcast_add_fusion
  38.8 5.6 %collective-permute-done.1 = f32[3,256,256]{1,2,0:T(8,128)S(1)} collective-permute-done((f32[3,256,256]{1,2,0:T(8,128)S(1)}, f32[3,256,256]{1,2,0:T(8,128)S(1)}, u32[]{:S(2)}, u32[]{:S(2)}) %collective-permute-start.1) | collective-permute-done | bytes 786464 | tf_op jit(solution)/shard_map/ppermute | solution.py:31
  46.0 1.5 collective-permute-start.14
  47.5 14.7 %collective-permute-done.7 = f32[128,2048]{1,0:T(8,128)S(1)} collective-permute-done((f32[128,2048]{1,0:T(8,128)S(1)}, f32[128,2048]{1,0:T(8,128)S(1)}, u32[]{:S(2)}, u32[]{:S(2)}) %collective-permute-start.7) | collective-permute-done | bytes 1048608 | tf_op jit(solution)/shard_map/ppermute | solution.py:31
  62.7 1.5 collective-permute-done.2
  65.6 16.2 %collective-permute-done.21 = f32[128,2048]{1,0:T(8,128)S(1)} collective-permute-done((f32[128,2048]{1,0:T(8,128)S(1)}, f32[128,2048]{1,0:T(8,128)S(1)}, u32[]{:S(2)}, u32[]{:S(2)}) %collective-permute-start.21) | collective-permute-done | bytes 1048608 | tf_op jit(solution)/shard_map/ppermute | solution.py:31
  82.3 22.1 %collective-permute-done.14 = f32[128,2048]{1,0:T(8,128)S(1)} collective-permute-done((f32[128,2048]{1,0:T(8,128)S(1)}, f32[128,2048]{1,0:T(8,128)S(1)}, u32[]{:S(2)}, u32[]{:S(2)}) %collective-permute-start.14) | collective-permute-done | bytes 1048608 | tf_op jit(solution)/shard_map/ppermute | solution.py:31
  105.1 7.2 %collective-permute-start.9 = (f32[128,2048]{1,0:T(8,128)S(1)}, f32[128,2048]{1,0:T(8,128)}, u32[]{:S(2)}, u32[]{:S(2)}) collective-permute-start(f32[128,2048]{1,0:T(8,128)S(1)} %add.233), channel_id=1, source_target_pairs={{0,4},{1,5},{2,6},{3,7},{4,0},{5,1},{6,2},{7,3},{8,12},{9,13},{10,... | collective-permute-start | bytes 3145736 | tf_op jit(solution)/shard_map/ppermute | solution.py:31
  113.3 2.3 collective-permute-start.4
  115.6 2.4 fusion.72
  119.3 2.5 fusion.62
  123.0 2.3 add.246
  125.7 1.4 add.241
  127.4 23.0 %collective-permute-done.4 = f32[3,256,256]{1,2,0:T(8,128)} collective-permute-done((f32[3,256,256]{1,2,0:T(8,128)}, f32[3,256,256]{1,2,0:T(8,128)}, u32[]{:S(2)}, u32[]{:S(2)}) %collective-permute-start.4) | collective-permute-done | bytes 786464 | tf_op jit(solution)/shard_map/ppermute | solution.py:31
  150.4 2.4 add.229
  155.3 2.8 reshape_reshape.9
  158.1 4.9 dynamic-slice_reduce_fusion.2
  164.1 1.8 collective-permute-start.10
  166.0 1.7 select_bitcast_fusion.1
  167.9 2.8 reshape_reshape.11
  172.3 2.8 reshape_reshape.10
  175.1 8.8 %dynamic-slice_reduce_fusion = (f32[256,4,256]{2,1,0:T(4,128)S(1)}, f32[256,4,256]{2,1,0:T(4,128)S(1)}) fusion(f32[256,4,2,256]{3,2,1,0:T(2,128)} %reshape_reshape.11, s32[]{:T(128)S(6)} %select_n.328, f32[256,4,2,256]{3,2,1,0:T(2,128)} %reshape_reshape.10), kind=kLoop, calls=%fused_computation.47 | loop fusion | bytes 4194308 | tf_op jit(solution)/shard_map/jit(dynamic_index_in_dim)/dynamic_slice | solution.py:131
  185.0 1.6 collective-permute-start.17
  187.8 2.1 collective-permute-start.24
  190.0 1.5 select_bitcast_fusion.7
  191.9 11.7 %cholesky.172 = f32[128,128]{1,0:T(8,128)S(1)} custom-call(f32[128,128]{1,0:T(8,128)S(1)} %cholesky.270), custom_call_target="Cholesky" | custom-call | tf_op jit(solution)/shard_map/jit(cholesky)/cholesky | solution.py:87
  203.7 9.8 %custom-call.15 = f32[1,128,128]{1,2,0:T(8,128)S(1)} custom-call(f32[1,128,128]{2,1,0:T(8,128)S(1)} %get-tuple-element.83), custom_call_target="InvertDiagBlocksLowerTriangular" | custom-call | tf_op jit(solution)/shard_map/jit(cholesky)/cholesky | solution.py:87
  213.9 11.7 %cholesky.189 = f32[128,128]{1,0:T(8,128)S(1)} custom-call(f32[128,128]{1,0:T(8,128)S(1)} %convolution_subtract_fusion.10), custom_call_target="Cholesky" | custom-call | tf_op jit(solution)/shard_map/jit(cholesky)/cholesky | solution.py:87
  227.7 3.8 while.6
  232.1 19.8 %custom-call.16 = f32[2,128,128]{1,2,0:T(8,128)S(1)} custom-call(f32[2,128,128]{2,1,0:T(8,128)S(1)} %get-tuple-element.24), custom_call_target="InvertDiagBlocksLowerTriangular" | custom-call | tf_op jit(solution)/shard_map/triangular_solve/custom-call.0 | solution.py:89
  255.5 11.7 %cholesky.206 = f32[128,128]{1,0:T(8,128)S(1)} custom-call(f32[128,128]{1,0:T(8,128)S(1)} %cholesky.273), custom_call_target="Cholesky" | custom-call | tf_op jit(solution)/shard_map/jit(cholesky)/cholesky | solution.py:87
  267.3 9.8 %custom-call.17 = f32[1,128,128]{1,2,0:T(8,128)S(1)} custom-call(f32[1,128,128]{2,1,0:T(8,128)S(1)} %get-tuple-element.79), custom_call_target="InvertDiagBlocksLowerTriangular" | custom-call | tf_op jit(solution)/shard_map/jit(cholesky)/cholesky | solution.py:87
  277.6 12.1 %cholesky.223 = f32[128,128]{1,0:T(8,128)S(1)} custom-call(f32[128,128]{1,0:T(8,128)S(1)} %convolution_subtract_fusion.9), custom_call_target="Cholesky" | custom-call | tf_op jit(solution)/shard_map/jit(cholesky)/cholesky | solution.py:87
  292.4 4.0 while.7
  296.4 19.7 %custom-call.18 = f32[2,128,128]{1,2,0:T(8,128)S(1)} custom-call(f32[2,128,128]{2,1,0:T(8,128)S(1)} %get-tuple-element.25), custom_call_target="InvertDiagBlocksLowerTriangular" | custom-call | tf_op jit(solution)/shard_map/triangular_solve/custom-call.0 | solution.py:89
  318.8 11.7 %cholesky.240 = f32[128,128]{1,0:T(8,128)S(1)} custom-call(f32[128,128]{1,0:T(8,128)S(1)} %cholesky.276), custom_call_target="Cholesky" | custom-call | tf_op jit(solution)/shard_map/jit(cholesky)/cholesky | solution.py:87
  330.6 9.8 %custom-call.19 = f32[1,128,128]{1,2,0:T(8,128)S(1)} custom-call(f32[1,128,128]{2,1,0:T(8,128)S(1)} %get-tuple-element.75), custom_call_target="InvertDiagBlocksLowerTriangular" | custom-call | tf_op jit(solution)/shard_map/jit(cholesky)/cholesky | solution.py:87
  340.9 11.7 %cholesky.257 = f32[128,128]{1,0:T(8,128)S(1)} custom-call(f32[128,128]{1,0:T(8,128)S(1)} %convolution_subtract_fusion.8), custom_call_target="Cholesky" | custom-call | tf_op jit(solution)/shard_map/jit(cholesky)/cholesky | solution.py:87
  354.1 3.8 fusion.32
  357.9 3.3 bitcast_subtract_fusion.1
  364.1 6.7 %while.8 = (s32[]{:T(128)}, f32[256,256]{1,0:T(8,128)S(1)}, s32[2,2]{1,0:T(2,128)}, f32[2,128,128]{2,1,0:T(8,128)}, s32[]{:T(128)}) while((s32[]{:T(128)}, f32[256,256]{1,0:T(8,128)S(1)}, s32[2,2]{1,0:T(2,128)}, f32[2,128,128]{2,1,0:T(8,128)}, s32[]{:T(128)}) %tuple.87), condition=%wide.while_cond.clone.1, body=%wide.while_body.clone.1.sunk | while | flops 2 | bytes 132205 | solution.py:89
  365.4 2.0 bitcast_dynamic-update-slice_fusion.14
  368.8 2.0 bitcast_dynamic-update-slice_fusion.14
  370.8 4.8 convolution_select_fusion.1
  375.6 20.5 %custom-call.20 = f32[2,128,128]{1,2,0:T(8,128)S(1)} custom-call(f32[2,128,128]{2,1,0:T(8,128)} %get-tuple-element.26), custom_call_target="InvertDiagBlocksLowerTriangular" | custom-call | tf_op jit(solution)/shard_map/triangular_solve/custom-call.0 | solution.py:89
  397.2 3.7 bitcast_subtract_fusion
  400.9 1.9 convolution_subtract_fusion
  406.8 3.3 convolution_select_fusion
  413.3 24.1 %collective-permute-done.12 = f32[256,1024]{1,0:T(8,128)S(1)} collective-permute-done((f32[256,1024]{1,0:T(8,128)S(1)}, f32[256,1024]{1,0:T(8,128)S(1)}, u32[]{:S(2)}, u32[]{:S(2)}) %collective-permute-start.12) | collective-permute-done | bytes 1048608 | tf_op jit(solution)/shard_map/ppermute | solution.py:31
  437.5 2.4 fusion.18
  442.0 15.3 %collective-permute-done.19 = f32[256,1024]{1,0:T(8,128)S(1)} collective-permute-done((f32[256,1024]{1,0:T(8,128)S(1)}, f32[256,1024]{1,0:T(8,128)S(1)}, u32[]{:S(2)}, u32[]{:S(2)}) %collective-permute-start.19) | collective-permute-done | bytes 1048608 | tf_op jit(solution)/shard_map/ppermute | solution.py:31
  457.3 2.5 convolution_select_fusion.3
  460.9 7.7 %collective-permute-done.26 = f32[256,1024]{1,0:T(8,128)S(1)} collective-permute-done((f32[256,1024]{1,0:T(8,128)S(1)}, f32[256,1024]{1,0:T(8,128)S(1)}, u32[]{:S(2)}, u32[]{:S(2)}) %collective-permute-start.26) | collective-permute-done | bytes 1048608 | tf_op jit(solution)/shard_map/ppermute | solution.py:31
  468.6 2.5 convolution_select_fusion.2
  472.1 2.1 fusion.8
  474.2 3.8 copy.12
  477.9 25.7 %subtract_select_fusion = f32[1024,2048]{1,0:T(8,128)} fusion(f32[1024,2048]{1,0:T(8,128)} %param.6, pred[2048]{0:T(1024)(128)(4,1)S(1)} %copy-done.28, pred[1024]{0:T(1024)(128)(4,1)S(1)} %copy-done.29, f32[256,2048]{1,0:T(8,128)} %convolution_select_fusion, f32[256,2048]{1,0:T(8,128)} %convolution_select_fusion.1, f32[256,2048]{1,0:T(8,128)S(1)} %fusion.32, ...), kind=kOutput, calls=%fused_computation.6 | convolution fusion | flops 19338362880 | bytes 26217472 | tf_op jit(solution)/shard_map/dot_general | solution.py:13
  (208 shorter events, 66.7 us)
Async XLA Ops:
  13.2 1.3 copy-start.7
  13.2 2.1 copy-start.4
  24.6 7.0 %collective-permute-start = (f32[3,256,256]{1,2,0:T(8,128)}, f32[3,256,256]{1,2,0:T(8,128)}, u32[]{:S(2)}, u32[]{:S(2)}) collective-permute-start(f32[3,256,256]{1,2,0:T(8,128)} %bitcast.219), channel_id=1, source_target_pairs={{0,4},{1,5},{2,6},{3,7},{4,0},{5,1},{6,2},{7,3},{8,12},{9,13},{10,... | collective-permute-start | bytes 2359304 | tf_op jit(solution)/shard_map/ppermute | solution.py:31
  25.3 4.0 copy-start.5
  27.7 6.8 %collective-permute-start.6 = (f32[128,2048]{1,0:T(8,128)}, f32[128,2048]{1,0:T(8,128)}, u32[]{:S(2)}, u32[]{:S(2)}) collective-permute-start(f32[128,2048]{1,0:T(8,128)} %dynamic-slice_bitcast_fusion.2), channel_id=1, source_target_pairs={{0,4},{1,5},{2,6},{3,7},{4,0},{5,1},{6,2},{7,3},{8,12},{9,13},{10,... | collective-permute-start | bytes 3145736 | tf_op jit(solution)/shard_map/ppermute | solution.py:31
  28.8 7.6 %collective-permute-start.20 = (f32[128,2048]{1,0:T(8,128)}, f32[128,2048]{1,0:T(8,128)}, u32[]{:S(2)}, u32[]{:S(2)}) collective-permute-start(f32[128,2048]{1,0:T(8,128)} %dynamic-slice_bitcast_fusion), channel_id=1, source_target_pairs={{0,4},{1,5},{2,6},{3,7},{4,0},{5,1},{6,2},{7,3},{8,12},{9,13},{10,... | collective-permute-start | bytes 3145736 | tf_op jit(solution)/shard_map/ppermute | solution.py:31
  30.4 14.3 %collective-permute-start.13 = (f32[128,2048]{1,0:T(8,128)}, f32[128,2048]{1,0:T(8,128)}, u32[]{:S(2)}, u32[]{:S(2)}) collective-permute-start(f32[128,2048]{1,0:T(8,128)} %dynamic-slice_bitcast_fusion.1), channel_id=1, source_target_pairs={{0,4},{1,5},{2,6},{3,7},{4,0},{5,1},{6,2},{7,3},{8,12},{9,13},{10,... | collective-permute-start | bytes 3145736 | tf_op jit(solution)/shard_map/ppermute | solution.py:31
  31.6 2.9 copy-start.8
  33.2 11.2 %collective-permute-start.1 = (f32[3,256,256]{1,2,0:T(8,128)S(1)}, f32[3,256,256]{1,2,0:T(8,128)S(1)}, u32[]{:S(2)}, u32[]{:S(2)}) collective-permute-start(f32[3,256,256]{1,2,0:T(8,128)S(1)} %bitcast_add_fusion.3), channel_id=1, source_target_pairs={{0,8},{1,9},{2,10},{3,11},{4,20},{5,21},{6,22},{7,23},{8,0},{9,1},... | collective-permute-start | bytes 2359304 | tf_op jit(solution)/shard_map/ppermute | solution.py:31
  35.9 8.8 %copy-start.6 = (f32[256,2048]{1,0:T(8,128)S(1)}, f32[256,2048]{1,0:T(8,128)}, u32[]{:S(2)}) copy-start(f32[256,2048]{1,0:T(8,128)} %copy-done.4) | copy-start | bytes 6291460
  35.9 26.3 %collective-permute-start.7 = (f32[128,2048]{1,0:T(8,128)S(1)}, f32[128,2048]{1,0:T(8,128)S(1)}, u32[]{:S(2)}, u32[]{:S(2)}) collective-permute-start(f32[128,2048]{1,0:T(8,128)S(1)} %bitcast_add_fusion.2), channel_id=1, source_target_pairs={{0,8},{1,9},{2,10},{3,11},{4,20},{5,21},{6,22},{7,23},{8,0},{9,1},... | collective-permute-start | bytes 3145736 | tf_op jit(solution)/shard_map/ppermute | solution.py:31
  37.9 44.0 %collective-permute-start.21 = (f32[128,2048]{1,0:T(8,128)S(1)}, f32[128,2048]{1,0:T(8,128)S(1)}, u32[]{:S(2)}, u32[]{:S(2)}) collective-permute-start(f32[128,2048]{1,0:T(8,128)S(1)} %bitcast_add_fusion), channel_id=1, source_target_pairs={{0,8},{1,9},{2,10},{3,11},{4,20},{5,21},{6,22},{7,23},{8,0},{9,1},... | collective-permute-start | bytes 3145736 | tf_op jit(solution)/shard_map/ppermute | solution.py:31
  44.5 19.6 %collective-permute-start.2 = (f32[3,256,256]{1,2,0:T(8,128)S(1)}, f32[3,256,256]{1,2,0:T(8,128)S(1)}, u32[]{:S(2)}, u32[]{:S(2)}) collective-permute-start(f32[3,256,256]{1,2,0:T(8,128)S(1)} %add.226), channel_id=1, source_target_pairs={{0,16},{1,17},{2,18},{3,19},{4,12},{5,13},{6,14},{7,15},{8,24},{9,... | collective-permute-start | bytes 2359304 | tf_op jit(solution)/shard_map/ppermute | solution.py:31
  46.0 58.4 %collective-permute-start.14 = (f32[128,2048]{1,0:T(8,128)S(1)}, f32[128,2048]{1,0:T(8,128)S(1)}, u32[]{:S(2)}, u32[]{:S(2)}) collective-permute-start(f32[128,2048]{1,0:T(8,128)S(1)} %bitcast_add_fusion.1), channel_id=1, source_target_pairs={{0,8},{1,9},{2,10},{3,11},{4,20},{5,21},{6,22},{7,23},{8,0},{9,1},... | collective-permute-start | bytes 3145736 | tf_op jit(solution)/shard_map/ppermute | solution.py:31
  62.3 42.6 %collective-permute-start.8 = (f32[128,2048]{1,0:T(8,128)S(1)}, f32[128,2048]{1,0:T(8,128)S(1)}, u32[]{:S(2)}, u32[]{:S(2)}) collective-permute-start(f32[128,2048]{1,0:T(8,128)S(1)} %add.232), channel_id=1, source_target_pairs={{0,16},{1,17},{2,18},{3,19},{4,12},{5,13},{6,14},{7,15},{8,24},{9,... | collective-permute-start | bytes 3145736 | tf_op jit(solution)/shard_map/ppermute | solution.py:31
  64.3 48.0 %collective-permute-start.3 = (f32[3,256,256]{1,2,0:T(8,128)S(1)}, f32[3,256,256]{1,2,0:T(8,128)S(1)}, u32[]{:S(2)}, u32[]{:S(2)}) collective-permute-start(f32[3,256,256]{1,2,0:T(8,128)S(1)} %add.227), channel_id=1, source_target_pairs={{0,1},{1,0},{2,3},{3,2},{4,5},{5,4},{6,7},{7,6},{8,9},{9,8},{10,11... | collective-permute-start | bytes 2359304 | tf_op jit(solution)/shard_map/ppermute | solution.py:31
  82.0 41.0 %collective-permute-start.22 = (f32[128,2048]{1,0:T(8,128)S(1)}, f32[128,2048]{1,0:T(8,128)}, u32[]{:S(2)}, u32[]{:S(2)}) collective-permute-start(f32[128,2048]{1,0:T(8,128)S(1)} %add.245), channel_id=1, source_target_pairs={{0,16},{1,17},{2,18},{3,19},{4,12},{5,13},{6,14},{7,15},{8,24},{9,... | collective-permute-start | bytes 3145736 | tf_op jit(solution)/shard_map/ppermute | solution.py:31
  104.5 21.1 %collective-permute-start.15 = (f32[128,2048]{1,0:T(8,128)S(1)}, f32[128,2048]{1,0:T(8,128)}, u32[]{:S(2)}, u32[]{:S(2)}) collective-permute-start(f32[128,2048]{1,0:T(8,128)S(1)} %add.240), channel_id=1, source_target_pairs={{0,16},{1,17},{2,18},{3,19},{4,12},{5,13},{6,14},{7,15},{8,24},{9,... | collective-permute-start | bytes 3145736 | tf_op jit(solution)/shard_map/ppermute | solution.py:31
  105.1 48.6 %collective-permute-start.9 = (f32[128,2048]{1,0:T(8,128)S(1)}, f32[128,2048]{1,0:T(8,128)}, u32[]{:S(2)}, u32[]{:S(2)}) collective-permute-start(f32[128,2048]{1,0:T(8,128)S(1)} %add.233), channel_id=1, source_target_pairs={{0,4},{1,5},{2,6},{3,7},{4,0},{5,1},{6,2},{7,3},{8,12},{9,13},{10,... | collective-permute-start | bytes 3145736 | tf_op jit(solution)/shard_map/ppermute | solution.py:31
  113.3 37.1 %collective-permute-start.4 = (f32[3,256,256]{1,2,0:T(8,128)}, f32[3,256,256]{1,2,0:T(8,128)}, u32[]{:S(2)}, u32[]{:S(2)}) collective-permute-start(f32[3,256,256]{1,2,0:T(8,128)} %add.228), channel_id=1, source_target_pairs={{0,2},{1,3},{2,0},{3,1},{4,6},{5,7},{6,4},{7,5},{8,10},{9,11},{10,... | collective-permute-start | bytes 2359304 | tf_op jit(solution)/shard_map/ppermute | solution.py:31
  125.3 40.6 %collective-permute-start.23 = (f32[128,2048]{1,0:T(8,128)}, f32[128,2048]{1,0:T(8,128)}, u32[]{:S(2)}, u32[]{:S(2)}) collective-permute-start(f32[128,2048]{1,0:T(8,128)} %add.246), channel_id=1, source_target_pairs={{0,4},{1,5},{2,6},{3,7},{4,0},{5,1},{6,2},{7,3},{8,12},{9,13},{10,... | collective-permute-start | bytes 3145736 | tf_op jit(solution)/shard_map/ppermute | solution.py:31
  125.6 126.6 %copy-start.15 = (f32[256,256]{1,0:T(8,128)}, f32[256,256]{1,0:T(8,128)S(1)}, u32[]{:S(2)}) copy-start(f32[256,256]{1,0:T(8,128)S(1)} %fusion.30) | copy-start | bytes 786436
  127.1 43.6 %collective-permute-start.16 = (f32[128,2048]{1,0:T(8,128)S(1)}, f32[128,2048]{1,0:T(8,128)}, u32[]{:S(2)}, u32[]{:S(2)}) collective-permute-start(f32[128,2048]{1,0:T(8,128)S(1)} %add.241), channel_id=1, source_target_pairs={{0,4},{1,5},{2,6},{3,7},{4,0},{5,1},{6,2},{7,3},{8,12},{9,13},{10,... | collective-permute-start | bytes 3145736 | tf_op jit(solution)/shard_map/ppermute | solution.py:31
  152.8 37.2 %collective-permute-start.5 = (f32[3,256,256]{1,2,0:T(8,128)}, f32[3,256,256]{1,2,0:T(8,128)}, u32[]{:S(2)}, u32[]{:S(2)}) collective-permute-start(f32[3,256,256]{1,2,0:T(8,128)} %add.229), channel_id=1, source_target_pairs={{0,4},{1,5},{2,6},{3,7},{4,0},{5,1},{6,2},{7,3},{8,12},{9,13},{10,... | collective-permute-start | bytes 2359304 | tf_op jit(solution)/shard_map/ppermute | solution.py:31
  155.3 2.8 copy-start.3
  164.1 232.0 %collective-permute-start.10 = (f32[256,1024]{1,0:T(8,128)}, f32[256,1024]{1,0:T(8,128)}, u32[]{:S(2)}, u32[]{:S(2)}) collective-permute-start(f32[256,1024]{1,0:T(8,128)} %bitcast.66), channel_id=1, source_target_pairs={{0,1},{5,6},{10,9},{15,14},{16,17},{21,22},{26,25},{31,30}} | collective-permute-start | bytes 3145736 | tf_op jit(solution)/shard_map/ppermute | solution.py:31
  167.9 2.8 copy-start
  172.3 2.8 copy-start.1
  185.0 217.9 %collective-permute-start.17 = (f32[256,1024]{1,0:T(8,128)}, f32[256,1024]{1,0:T(8,128)}, u32[]{:S(2)}, u32[]{:S(2)}) collective-permute-start(f32[256,1024]{1,0:T(8,128)} %bitcast.68), channel_id=1, source_target_pairs={{0,1},{5,6},{10,9},{15,14},{16,17},{21,22},{26,25},{31,30}} | collective-permute-start | bytes 3145736 | tf_op jit(solution)/shard_map/ppermute | solution.py:31
  187.8 216.2 %collective-permute-start.24 = (f32[256,1024]{1,0:T(8,128)}, f32[256,1024]{1,0:T(8,128)}, u32[]{:S(2)}, u32[]{:S(2)}) collective-permute-start(f32[256,1024]{1,0:T(8,128)} %bitcast.70), channel_id=1, source_target_pairs={{0,1},{5,6},{10,9},{15,14},{16,17},{21,22},{26,25},{31,30}} | collective-permute-start | bytes 3145736 | tf_op jit(solution)/shard_map/ppermute | solution.py:31
  231.5 0.6 copy-start.30
  252.8 101.2 %copy-start.18 = (f32[128,256]{1,0:T(8,128)}, f32[128,256]{1,0:T(8,128)S(1)}, u32[]{:S(2)}) copy-start(f32[128,256]{1,0:T(8,128)S(1)} %fusion.48) | copy-start | bytes 393220
  254.0 103.8 %copy-start.9 = (f32[256,256]{1,0:T(8,128)}, f32[256,256]{1,0:T(8,128)S(1)}, u32[]{:S(2)}) copy-start(f32[256,256]{1,0:T(8,128)S(1)} %fusion.26) | copy-start | bytes 786436
  255.3 37.1 %copy-start.31 = (s32[2,2]{1,0:T(2,128)S(1)}, s32[2,2]{1,0:T(2,128)}, u32[]{:S(2)}) copy-start(s32[2,2]{1,0:T(2,128)} %copy-done.30) | copy-start | bytes 52
  255.3 60.7 %copy-start.16 = (f32[256,256]{1,0:T(8,128)S(1)}, f32[256,256]{1,0:T(8,128)}, u32[]{:S(2)}) copy-start(f32[256,256]{1,0:T(8,128)} %copy-done.15) | copy-start | bytes 786436
  316.4 54.4 %copy-start.20 = (f32[128,256]{1,0:T(8,128)}, f32[128,256]{1,0:T(8,128)S(1)}, u32[]{:S(2)}) copy-start(f32[128,256]{1,0:T(8,128)S(1)} %fusion.35) | copy-start | bytes 393220
  317.0 0.7 copy-start.22
  318.2 82.7 %copy-start.13 = (f32[256,256]{1,0:T(8,128)}, f32[256,256]{1,0:T(8,128)S(1)}, u32[]{:S(2)}) copy-start(f32[256,256]{1,0:T(8,128)S(1)} %fusion.31) | copy-start | bytes 786436
  353.4 0.7 copy-start.25
  354.1 3.8 copy-start.2
  357.9 12.9 %copy-start.23 = (f32[128,256]{1,0:T(8,128)S(1)}, f32[128,256]{1,0:T(8,128)}, u32[]{:S(2)}) copy-start(f32[128,256]{1,0:T(8,128)} %copy-done.22) | copy-start | bytes 393220
  396.1 4.8 copy-start.26
  396.1 8.9 %collective-permute-start.11 = (f32[256,1024]{1,0:T(8,128)}, f32[256,1024]{1,0:T(8,128)S(1)}, u32[]{:S(2)}, u32[]{:S(2)}) collective-permute-start(f32[256,1024]{1,0:T(8,128)} %collective-permute-done.10), channel_id=1, source_target_pairs={{1,2},{6,7},{9,8},{14,13},{17,18},{22,23},{25,24},{30,29}} | collective-permute-start | bytes 3145736 | tf_op jit(solution)/shard_map/ppermute | solution.py:31
  397.2 3.7 copy-start.12
  402.9 3.6 copy-start.27
  402.9 7.2 %collective-permute-start.18 = (f32[256,1024]{1,0:T(8,128)}, f32[256,1024]{1,0:T(8,128)S(1)}, u32[]{:S(2)}, u32[]{:S(2)}) collective-permute-start(f32[256,1024]{1,0:T(8,128)} %collective-permute-done.17), channel_id=1, source_target_pairs={{1,2},{6,7},{9,8},{14,13},{17,18},{22,23},{25,24},{30,29}} | collective-permute-start | bytes 3145736 | tf_op jit(solution)/shard_map/ppermute | solution.py:31
  404.1 7.7 %collective-permute-start.25 = (f32[256,1024]{1,0:T(8,128)}, f32[256,1024]{1,0:T(8,128)S(1)}, u32[]{:S(2)}, u32[]{:S(2)}) collective-permute-start(f32[256,1024]{1,0:T(8,128)} %collective-permute-done.24), channel_id=1, source_target_pairs={{1,2},{6,7},{9,8},{14,13},{17,18},{22,23},{25,24},{30,29}} | collective-permute-start | bytes 3145736 | tf_op jit(solution)/shard_map/ppermute | solution.py:31
  405.2 32.3 %collective-permute-start.12 = (f32[256,1024]{1,0:T(8,128)S(1)}, f32[256,1024]{1,0:T(8,128)S(1)}, u32[]{:S(2)}, u32[]{:S(2)}) collective-permute-start(f32[256,1024]{1,0:T(8,128)S(1)} %broadcast_select_fusion.2), channel_id=1, source_target_pairs={{2,3},{5,4},{10,11},{13,12},{18,19},{21,20},{26,27},{29,28}} | collective-permute-start | bytes 3145736 | tf_op jit(solution)/shard_map/ppermute | solution.py:31
  410.3 27.2 %copy-start.19 = (f32[128,256]{1,0:T(8,128)S(1)}, f32[128,256]{1,0:T(8,128)}, u32[]{:S(2)}) copy-start(f32[128,256]{1,0:T(8,128)} %copy-done.18) | copy-start | bytes 393220
  410.3 47.0 %collective-permute-start.19 = (f32[256,1024]{1,0:T(8,128)S(1)}, f32[256,1024]{1,0:T(8,128)S(1)}, u32[]{:S(2)}, u32[]{:S(2)}) collective-permute-start(f32[256,1024]{1,0:T(8,128)S(1)} %broadcast_select_fusion.1), channel_id=1, source_target_pairs={{2,3},{5,4},{10,11},{13,12},{18,19},{21,20},{26,27},{29,28}} | collective-permute-start | bytes 3145736 | tf_op jit(solution)/shard_map/ppermute | solution.py:31
  411.9 28.0 %copy-start.10 = (f32[256,256]{1,0:T(8,128)S(1)}, f32[256,256]{1,0:T(8,128)}, u32[]{:S(2)}) copy-start(f32[256,256]{1,0:T(8,128)} %copy-done.9) | copy-start | bytes 786436
  411.9 56.6 %collective-permute-start.26 = (f32[256,1024]{1,0:T(8,128)S(1)}, f32[256,1024]{1,0:T(8,128)S(1)}, u32[]{:S(2)}, u32[]{:S(2)}) collective-permute-start(f32[256,1024]{1,0:T(8,128)S(1)} %broadcast_select_fusion), channel_id=1, source_target_pairs={{2,3},{5,4},{10,11},{13,12},{18,19},{21,20},{26,27},{29,28}} | collective-permute-start | bytes 3145736 | tf_op jit(solution)/shard_map/ppermute | solution.py:31
  439.9 17.4 %copy-start.21 = (f32[128,256]{1,0:T(8,128)S(1)}, f32[128,256]{1,0:T(8,128)}, u32[]{:S(2)}) copy-start(f32[128,256]{1,0:T(8,128)} %copy-done.20) | copy-start | bytes 393220
  439.9 17.4 %copy-start.24 = (f32[128,256]{1,0:T(8,128)S(1)}, f32[128,256]{1,0:T(8,128)}, u32[]{:S(2)}) copy-start(f32[128,256]{1,0:T(8,128)} %copy-done.22) | copy-start | bytes 393220
  457.3 2.5 copy-start.14
  459.9 11.2 %copy-start.11 = (f32[256,1024]{1,0:T(8,128)}, f32[256,1024]{1,0:T(8,128)S(1)}, u32[]{:S(2)}) copy-start(f32[256,1024]{1,0:T(8,128)S(1)} %convolution_select_fusion.3) | copy-start | bytes 3145732
  471.1 1.0 copy-start.17
  474.2 3.8 copy-start.28
  474.2 3.8 copy-start.29
